TPU v7x, 32 devices: a whole 2x2x4 slice. The times are simulated.
32 devices in a mesh: dp: 8 (over z, x), tp: 4 (over y, core).
Axes of the slice: x: 2, y: 2, z: 4, core: 2. Of those that a mesh axis runs over, the one named last changes fastest.
Arguments:
- layer_input: bfloat16 [8, 1024, 768], P('dp', 'tp'), may hold values from -6 to 6
- lengths: int32 [8], P('dp'), may hold values from 8 to 1024, as said below
- w_qkv: bfloat16 [768, 3, 768], P(None, None, 'tp'), may hold values from -0.21875 to 0.21875
- w_out: bfloat16 [768, 768], P('tp'), may hold values from -1.75 to 1.75
- w_gate: bfloat16 [768, 3072], P(None, 'tp'), may hold values from -0.21875 to 0.21875
- w_up: bfloat16 [768, 3072], P(None, 'tp'), may hold values from -0.21875 to 0.21875
- w_down: bfloat16 [3072, 768], P('tp'), may hold values from -0.109375 to 0.109375
- gain_one: float32 [768], replicated, may hold values from 0.5 to 1.5
- bias_one: float32 [768], replicated, may hold values from -1.8 to 1.8
- gain_two: float32 [768], replicated, may hold values from 0.5 to 1.5
- bias_two: float32 [768], replicated, may hold values from -1.8 to 1.8
- cotangent: bfloat16 [8, 1024, 768], P('dp', 'tp'), may hold values from -6 to 6
Outputs:
- output: bfloat16 [8, 1024, 768], P('dp', 'tp')
- input_grad: float32 [8, 1024, 768], P('dp', 'tp')
- qkv_grad: float32 [768, 3, 768], P('dp', None, 'tp')
- out_grad: float32 [768, 768], P('tp', 'dp')
- gate_grad: float32 [768, 3072], P('dp', 'tp')
- up_grad: float32 [768, 3072], P('dp', 'tp')
- down_grad: float32 [3072, 768], P('tp', 'dp')
- gain_one_grad: float32 [768], replicated
- bias_one_grad: float32 [768], replicated
- gain_two_grad: float32 [768], replicated
- bias_two_grad: float32 [768], replicated
Inputs may be any that keep to these rules, and one draw needn't show every extreme that they name: `lengths`: each row's count of real tokens; later positions of the row are padding. Some row has exactly 1024 and some row exactly 8.
All inputs are finite; a program needn't handle non-finite values.
Results may differ from a plain program's by a relative error of at most 0.017.
Values may be sent and summed in bfloat16 or wider, within the bound.
No kernel may reach another device: no remote copies, remote signals or barrier semaphores. Data moves between devices by JAX's collectives and lax.ppermute only.
A program may use at most 128 MiB of HBM per device.

v0:
```python
import jax
import jax.numpy as jnp
from jax import lax
from jax.sharding import PartitionSpec as P

HD = 64
masked_score = -1e30
epsilon = 1e-05


def angle_tables(positions_count, head_width):
    position = jnp.arange(positions_count, dtype=jnp.float32)
    frequency = 1000.0 ** (-jnp.arange(head_width // 2, dtype=jnp.float32) * 2.0 / head_width)
    angles = position[:, None] * frequency[None, :]
    return (jnp.cos(angles)[:, None, :], jnp.sin(angles)[:, None, :])


def rotate(values, cosine, sine_table, direction):
    half_width = values.shape[-1] // 2
    lower = values[..., :half_width]
    upper = values[..., half_width:]
    return jnp.concatenate(
        [
            lower * cosine - direction * upper * sine_table,
            upper * cosine + direction * lower * sine_table,
        ],
        axis=-1,
    )


def norm_forward(values, gain_vec, bias_vec):
    center = values - jnp.mean(values, axis=-1, keepdims=True)
    inverse = lax.rsqrt(jnp.mean(center * center, axis=-1, keepdims=True) + epsilon)
    normed = center * inverse
    return (normed * gain_vec + bias_vec, normed, inverse)


def norm_backward(upstream, normed, inverse, gain_vec):
    scaled = upstream * gain_vec
    grad_values = inverse * (
        scaled
        - jnp.mean(scaled, axis=-1, keepdims=True)
        - normed * jnp.mean(scaled * normed, axis=-1, keepdims=True)
    )
    gain_part = jnp.sum(upstream * normed, axis=(0, 1))
    bias_part = jnp.sum(upstream, axis=(0, 1))
    return (grad_values, gain_part, bias_part)


def body(
    layer_input,
    lengths,
    w_qkv,
    w_out,
    w_gate,
    w_up,
    w_down,
    gain_one,
    bias_one,
    gain_two,
    bias_two,
    cotangent,
):
    row_count, piece_len, model_width = layer_input.shape
    local_width = w_qkv.shape[2]
    heads_local = local_width // HD
    seq_len = piece_len * lax.axis_size("tp")
    offset = lax.axis_index("tp") * piece_len
    scale = HD ** (-0.5)
    key_valid = jnp.arange(seq_len, dtype=jnp.int32)[None, :] < lengths[:, None]
    own_positions = offset + jnp.arange(piece_len, dtype=jnp.int32)
    row_valid = (own_positions[None, :] < lengths[:, None]).astype(jnp.float32)
    cosine, sine_table = angle_tables(seq_len, HD)
    gathered = lax.all_gather(layer_input, "tp", axis=1, tiled=True)
    projected = jnp.einsum("rsd,dce->rsce", gathered, w_qkv, preferred_element_type=jnp.float32)
    shaped = projected.reshape(row_count, seq_len, 3, heads_local, HD)
    queries = rotate(shaped[:, :, 0], cosine, sine_table, 1.0).astype(jnp.bfloat16)
    keys_rot = rotate(shaped[:, :, 1], cosine, sine_table, 1.0).astype(jnp.bfloat16)
    values_low = shaped[:, :, 2].astype(jnp.bfloat16)

    def attend(operands):
        query_row, keys_row, values_row, valid_row = operands
        scores = (
            jnp.einsum("she,the->hst", query_row, keys_row, preferred_element_type=jnp.float32)
            * scale
        )
        scores = jnp.where(valid_row[None, None, :], scores, masked_score)
        row_max = jnp.max(scores, axis=-1, keepdims=True)
        exps_raw = jnp.exp(scores - row_max)
        row_total = jnp.sum(exps_raw, axis=-1, keepdims=True)
        attn_probs = (exps_raw / row_total).astype(jnp.bfloat16)
        mixed = jnp.einsum(
            "hst,the->she", attn_probs, values_row, preferred_element_type=jnp.float32
        )
        return (mixed.astype(jnp.bfloat16), (row_max + jnp.log(row_total))[..., 0])

    heads_out, log_total = lax.map(attend, (queries, keys_rot, values_low, key_valid))
    heads_flat = heads_out.reshape(row_count, seq_len, local_width)
    attn_partial = jnp.einsum("rsk,kd->rsd", heads_flat, w_out, preferred_element_type=jnp.float32)
    attn_out = lax.psum_scatter(attn_partial, "tp", scatter_dimension=1, tiled=True)
    first_norm, normed_one, inverse_one = norm_forward(
        layer_input.astype(jnp.float32) + attn_out, gain_one, bias_one
    )
    first_low = first_norm.astype(jnp.bfloat16)
    gate_full, up_full, down_full = (w_gate, w_up, w_down)
    ffn_input = lax.all_gather(first_low, "tp", axis=1, tiled=True)
    gate_act = jnp.einsum("rsd,df->rsf", ffn_input, gate_full, preferred_element_type=jnp.float32)
    up_act = jnp.einsum("rsd,df->rsf", ffn_input, up_full, preferred_element_type=jnp.float32)
    sigmoid_gate = jax.nn.sigmoid(gate_act)
    hidden = (gate_act * sigmoid_gate * up_act).astype(jnp.bfloat16)
    ffn_partial = jnp.einsum("rsf,fd->rsd", hidden, down_full, preferred_element_type=jnp.float32)
    ffn_out = lax.psum_scatter(
        ffn_partial.astype(jnp.bfloat16), "tp", scatter_dimension=1, tiled=True
    ).astype(jnp.float32)
    second_out, normed_two, inverse_two = norm_forward(first_norm + ffn_out, gain_two, bias_two)
    output = (second_out * row_valid[:, :, None]).astype(jnp.bfloat16)
    grad_output = cotangent.astype(jnp.float32) * row_valid[:, :, None]
    grad_second, gain_two_part, bias_two_part = norm_backward(
        grad_output, normed_two, inverse_two, gain_two
    )
    grad_second_low = grad_second.astype(jnp.bfloat16)
    grad_ffn = lax.all_gather(grad_second_low, "tp", axis=1, tiled=True)
    down_grad = jnp.einsum("rsf,rsd->fd", hidden, grad_ffn, preferred_element_type=jnp.float32)
    grad_hidden = jnp.einsum("rsd,fd->rsf", grad_ffn, down_full, preferred_element_type=jnp.float32)
    grad_gate = (
        grad_hidden * up_act * sigmoid_gate * (1.0 + gate_act * (1.0 - sigmoid_gate))
    ).astype(jnp.bfloat16)
    grad_up = (grad_hidden * gate_act * sigmoid_gate).astype(jnp.bfloat16)
    gate_grad = jnp.einsum("rsd,rsf->df", ffn_input, grad_gate, preferred_element_type=jnp.float32)
    up_grad = jnp.einsum("rsd,rsf->df", ffn_input, grad_up, preferred_element_type=jnp.float32)
    grad_inner = jnp.einsum(
        "rsf,df->rsd", grad_gate, gate_full, preferred_element_type=jnp.float32
    ) + jnp.einsum("rsf,df->rsd", grad_up, up_full, preferred_element_type=jnp.float32)
    grad_first_part = lax.psum_scatter(grad_inner, "tp", scatter_dimension=1, tiled=True)
    grad_first = grad_second + grad_first_part
    grad_res, gain_one_part, bias_one_part = norm_backward(
        grad_first, normed_one, inverse_one, gain_one
    )
    grad_attn = lax.all_gather(grad_res.astype(jnp.bfloat16), "tp", axis=1, tiled=True)
    out_grad = jnp.einsum("rsk,rsd->kd", heads_flat, grad_attn, preferred_element_type=jnp.float32)
    grad_heads = jnp.einsum("rsd,kd->rsk", grad_attn, w_out, preferred_element_type=jnp.float32)
    grad_heads = grad_heads.astype(jnp.bfloat16).reshape(row_count, seq_len, heads_local, HD)

    def attend_back(operands):
        query_row, keys_row, values_row, valid_row, total_row, grad_row = operands
        scores = (
            jnp.einsum("she,the->hst", query_row, keys_row, preferred_element_type=jnp.float32)
            * scale
        )
        scores = jnp.where(valid_row[None, None, :], scores, masked_score)
        attn_probs = jnp.exp(scores - total_row[:, :, None])
        grad_probs = jnp.einsum(
            "she,the->hst", grad_row, values_row, preferred_element_type=jnp.float32
        )
        delta = jnp.sum(attn_probs * grad_probs, axis=-1, keepdims=True)
        grad_scores = (attn_probs * (grad_probs - delta)).astype(jnp.bfloat16)
        grad_query = (
            jnp.einsum("hst,the->she", grad_scores, keys_row, preferred_element_type=jnp.float32)
            * scale
        )
        grad_keys = (
            jnp.einsum("hst,she->the", grad_scores, query_row, preferred_element_type=jnp.float32)
            * scale
        )
        grad_values = jnp.einsum(
            "hst,she->the",
            attn_probs.astype(jnp.bfloat16),
            grad_row,
            preferred_element_type=jnp.float32,
        )
        return (grad_query, grad_keys, grad_values)

    grad_query, grad_keys, grad_values = lax.map(
        attend_back, (queries, keys_rot, values_low, key_valid, log_total, grad_heads)
    )
    grad_qkv = jnp.stack(
        [
            rotate(grad_query, cosine, sine_table, -1.0),
            rotate(grad_keys, cosine, sine_table, -1.0),
            grad_values,
        ],
        axis=2,
    )
    grad_qkv = grad_qkv.reshape(row_count, seq_len, 3, local_width).astype(jnp.bfloat16)
    qkv_grad = jnp.einsum("rsd,rsce->dce", gathered, grad_qkv, preferred_element_type=jnp.float32)
    grad_gathered = jnp.einsum("rsce,dce->rsd", grad_qkv, w_qkv, preferred_element_type=jnp.float32)
    input_grad = grad_res + lax.psum_scatter(
        grad_gathered.astype(jnp.bfloat16), "tp", scatter_dimension=1, tiled=True
    ).astype(jnp.float32)
    qkv_grad, out_grad, gate_grad, up_grad, down_grad = (
        lax.psum_scatter(qkv_grad, "dp", scatter_dimension=0, tiled=True),
        lax.psum_scatter(out_grad, "dp", scatter_dimension=1, tiled=True),
        lax.psum_scatter(gate_grad, "dp", scatter_dimension=0, tiled=True),
        lax.psum_scatter(up_grad, "dp", scatter_dimension=0, tiled=True),
        lax.psum_scatter(down_grad, "dp", scatter_dimension=1, tiled=True),
    )
    gain_one_grad, bias_one_grad, gain_two_grad, bias_two_grad = lax.psum(
        (gain_one_part, bias_one_part, gain_two_part, bias_two_part), ("dp", "tp")
    )
    return (
        output,
        input_grad,
        qkv_grad,
        out_grad,
        gate_grad,
        up_grad,
        down_grad,
        gain_one_grad,
        bias_one_grad,
        gain_two_grad,
        bias_two_grad,
    )


def solution(mesh):
    placed = (
        P("dp", "tp", None),
        P("dp"),
        P(None, None, "tp"),
        P("tp", None),
        P(None, "tp"),
        P(None, "tp"),
        P("tp", None),
        P(),
        P(),
        P(),
        P(),
        P("dp", "tp", None),
    )
    return jax.shard_map(
        body,
        mesh=mesh,
        in_specs=placed,
        out_specs=(
            P("dp", "tp", None),
            P("dp", "tp", None),
            P("dp", None, "tp"),
            P("tp", "dp"),
            P("dp", "tp"),
            P("dp", "tp"),
            P("tp", "dp"),
            P(),
            P(),
            P(),
            P(),
        ),
        check_vma=False,
    )
```

profile of v0, /device:TPU:0, one launch (start us, length us, event | category | flops | bytes accessed | tf_op | source)
XLA Modules:
  0.0 658.0 jit_solution(8090936462190204073)
XLA Ops:
  8.6 1.2 broadcast_multiply_fusion
  9.8 22.1 %all-gather.5.cloned.1.call-done = bf16[1,1024,768]{2,1,0:T(8,128)(2,1)} async-done(((bf16[1,256,768]{2,1,0:T(8,128)(2,1)}), bf16[1,1024,768]{2,1,0:T(8,128)(2,1)}) %all-gather.5.cloned.1.call-update) | async-done | bytes 1572880 | tf_op jit(solution)/shard_map/all_gather | solution.py:74
  32.0 2.7 convolution_bitcast_fusion.1
  35.1 2.4 fusion.64
  37.5 1.7 fusion
  39.3 2.8 copy-done.2
  42.1 2.3 fusion.38
  45.2 2.3 convolution_bitcast_fusion
  47.5 38.0 %reduce-scatter.14.cloned.1.call-done = f32[1,256,768]{2,1,0:T(8,128)} async-done(((f32[1,1024,768]{2,1,0:T(8,128)}), f32[1,256,768]{2,1,0:T(8,128)}) %reduce-scatter.14.cloned.1.call-update) | async-done | bytes 786448 | tf_op jit(solution)/shard_map/reduce_scatter | solution.py:100
  85.5 1.3 fusion.63
  88.1 19.7 %all-gather.7.cloned.1.call-done = bf16[1,1024,768]{2,1,0:T(8,128)(2,1)} async-done(((bf16[1,256,768]{2,1,0:T(8,128)(2,1)}), bf16[1,1024,768]{2,1,0:T(8,128)(2,1)}) %all-gather.7.cloned.1.call-update) | async-done | bytes 1572880 | tf_op jit(solution)/shard_map/all_gather | solution.py:106
  107.9 3.3 fusion.23
  111.2 5.4 multiply_convert_fusion.3
  116.6 1.2 copy-done.45
  117.8 2.5 fusion.25
  120.6 27.9 %reduce-scatter.16.cloned.1.call-done = bf16[1,256,768]{2,1,0:T(8,128)(2,1)} async-done(((bf16[1,1024,768]{2,1,0:T(8,128)(2,1)}), bf16[1,256,768]{2,1,0:T(8,128)(2,1)}) %reduce-scatter.16.cloned.1.call-update) | async-done | bytes 393232 | tf_op jit(solution)/shard_map/reduce_scatter | solution.py:112
  148.5 1.3 fusion.62
  152.3 19.7 %all-gather.9.cloned.1.call-done = bf16[1,1024,768]{2,1,0:T(8,128)(2,1)} async-done(((bf16[1,256,768]{2,1,0:T(8,128)(2,1)}), bf16[1,1024,768]{2,1,0:T(8,128)(2,1)}) %all-gather.9.cloned.1.call-update) | async-done | bytes 1572880 | tf_op jit(solution)/shard_map/all_gather | solution.py:122
  172.0 5.4 multiply_convert_fusion.1
  177.5 1.4 fusion.65
  179.6 3.1 add_bitcast_fusion
  182.8 38.0 %reduce-scatter.18.cloned.1.call-done = f32[1,256,768]{2,1,0:T(8,128)} async-done(((f32[1,1024,768]{2,1,0:T(8,128)}), f32[1,256,768]{2,1,0:T(8,128)}) %reduce-scatter.18.cloned.1.call-update) | async-done | bytes 786448 | tf_op jit(solution)/shard_map/reduce_scatter | solution.py:134
  220.8 3.2 multiply_reduce_fusion.2
  224.0 1.7 fusion.60
  225.9 19.7 %all-gather.11.cloned.1.call-done = bf16[1,1024,768]{2,1,0:T(8,128)(2,1)} async-done(((bf16[1,256,768]{2,1,0:T(8,128)(2,1)}), bf16[1,1024,768]{2,1,0:T(8,128)(2,1)}) %all-gather.11.cloned.1.call-update) | async-done | bytes 1572880 | tf_op jit(solution)/shard_map/all_gather | solution.py:139
  245.6 2.1 fusion.32
  247.7 6.3 multiply_reduce_fusion
  256.2 5.3 multiply_convert_fusion
  261.5 5.0 fusion.27
  266.5 1.2 fusion.28
  267.9 1.6 fusion.29
  270.0 6.7 %fusion.35 = bf16[3,64,1024]{2,1,0:T(8,128)(2,1)S(1)} fusion(bf16[1024,3,64]{0,2,1:T(8,128)(2,1)S(1)} %bitcast.125, f32[3,1024,1024]{1,2,0:T(8,128)} %copy-done.2, f32[3,1024]{1,0:T(4,128)S(1)} %log_add_fusion), kind=kOutput, calls=%fused_computation.47 | convolution fusion | flops 409141248 | bytes 13381632 | tf_op jit(solution)/shard_map/while/body/eval_jaxpr/hst,she->the/dot_general | solution.py:165
  276.7 2.6 fusion.26
  279.3 3.7 fusion.7
  283.1 3.0 copy.42
  286.4 4.3 fusion.13
  290.7 1.3 copy-done.19
  292.0 4.3 fusion.17
  296.4 1.3 copy-done.40
  297.8 4.3 fusion.19
  302.8 39.8 %all-reduce = (f32[768]{0:T(1024)}, f32[768]{0:T(1024)}, f32[768]{0:T(1024)}, f32[768]{0:T(1024)}) all-reduce(f32[768]{0:T(1024)S(1)} %copy-done.36, f32[768]{0:T(1024)S(1)} %copy-done.37, f32[768]{0:T(1024)S(1)} %copy-done.34, f32[768]{0:T(1024)S(1)} %copy-done.35), channel_id=1, replica_groups=mesh['dp'=8,'tp'=4] {'dp','tp'}, use_global_device_ids=true, to_apply=%region_21.22 | all-reduce | flops 3072 | bytes 24576 | tf_op jit(solution)/shard_map/psum | solution.py:197
  342.6 1.6 copy.41
  344.2 18.5 %reduce-scatter.20.cloned.1.call-done = bf16[1,256,768]{2,1,0:T(8,128)(2,1)} async-done(((bf16[1,1024,768]{2,1,0:T(8,128)(2,1)}), bf16[1,256,768]{2,1,0:T(8,128)(2,1)}) %reduce-scatter.20.cloned.1.call-update) | async-done | bytes 393232 | tf_op jit(solution)/shard_map/reduce_scatter | solution.py:187
  362.7 1.9 convert_add_fusion
  364.6 68.7 %reduce-scatter.28.cloned.1.call-done = f32[96,576]{1,0:T(8,128)} async-done(((f32[768,576]{1,0:T(8,128)}), f32[96,576]{1,0:T(8,128)}) %reduce-scatter.28.cloned.1.call-update) | async-done | bytes 221200
  435.3 70.7 %reduce-scatter.26.cloned.1.call-done = f32[768,96]{0,1:T(8,128)} async-done(((f32[768,768]{0,1:T(8,128)}), f32[768,96]{0,1:T(8,128)}) %reduce-scatter.26.cloned.1.call-update) | async-done | bytes 294928 | tf_op jit(solution)/shard_map/reduce_scatter | solution.py:195
  506.0 72.6 %reduce-scatter.24.cloned.1.call-done = f32[96,768]{1,0:T(8,128)} async-done(((f32[768,768]{1,0:T(8,128)}), f32[96,768]{1,0:T(8,128)}) %reduce-scatter.24.cloned.1.call-update) | async-done | bytes 294928 | tf_op jit(solution)/shard_map/reduce_scatter | solution.py:194
  578.7 72.8 %reduce-scatter.22.cloned.1.call-done = f32[96,768]{1,0:T(8,128)} async-done(((f32[768,768]{1,0:T(8,128)}), f32[96,768]{1,0:T(8,128)}) %reduce-scatter.22.cloned.1.call-update) | async-done | bytes 294928 | tf_op jit(solution)/shard_map/reduce_scatter | solution.py:193
  (147 shorter events, 12.7 us)
Async XLA Ops:
  7.2 110.6 %copy-start = (bf16[768,768]{1,0:T(8,128)(2,1)S(1)}, bf16[768,768]{1,0:T(8,128)(2,1)}, u32[]{:S(2)}) copy-start(bf16[768,768]{1,0:T(8,128)(2,1)} %param.18) | copy-start | bytes 3538948
  7.2 24.8 %all-gather.5.cloned.1.call-start = ((), (), s32[]{:S(2)}) async-start(), calls=%async_computation.9 | async-start | bytes 1966080 | tf_op jit(solution)/shard_map/all_gather | solution.py:74
  7.9 77.6 %reduce-scatter.14.cloned.1.call-start = ((), (), s32[]{:S(2)}) async-start(), calls=%async_computation.10 | async-start | bytes 3932160 | tf_op jit(solution)/shard_map/reduce_scatter | solution.py:100
  9.8 25.0 %copy-start.21 = (f32[1024,32]{0,1:T(8,128)}, f32[1024,32]{0,1:T(8,128)S(1)}, u32[]{:S(2)}) copy-start(f32[1024,32]{0,1:T(8,128)S(1)} %get-tuple-element.122) | copy-start | bytes 393220
  34.7 4.6 copy-start.5
  35.1 2.4 copy-start.6
  35.1 2.4 copy-start.8
  35.1 2.4 copy-start.10
  35.1 2.4 copy-start.12
  37.5 4.6 copy-start.2
  42.1 2.3 copy-start.28
  42.1 3.1 copy-start.24
  47.5 38.1 %copy-start.14 = (bf16[1,256,768]{2,1,0:T(8,128)(2,1)S(1)}, bf16[1,256,768]{2,1,0:T(8,128)(2,1)}, u32[]{:S(2)}) copy-start(bf16[1,256,768]{2,1,0:T(8,128)(2,1)} %param.12) | copy-start | bytes 1179652
  47.5 39.6 %copy-start.26 = (f32[768]{0:T(1024)S(1)}, f32[768]{0:T(1024)}, u32[]{:S(2)}) copy-start(f32[768]{0:T(1024)} %param.19) | copy-start | bytes 9220
  47.5 39.6 %copy-start.33 = (f32[768]{0:T(1024)S(1)}, f32[768]{0:T(1024)}, u32[]{:S(2)}) copy-start(f32[768]{0:T(1024)} %param.20) | copy-start | bytes 9220
  47.5 60.4 %all-gather.7.cloned.1.call-start = ((), (), s32[]{:S(2)}) async-start(), calls=%async_computation.11 | async-start | bytes 1966080 | tf_op jit(solution)/shard_map/all_gather | solution.py:106
  86.8 134.0 %copy-start.31 = (f32[256]{0:T(256)}, f32[256]{0:T(256)S(1)}, u32[]{:S(2)}) copy-start(f32[256]{0:T(256)S(1)} %broadcast_multiply_fusion.6) | copy-start | bytes 3076
  87.1 133.7 %copy-start.32 = (f32[256]{0:T(256)}, f32[256]{0:T(256)S(1)}, u32[]{:S(2)}) copy-start(f32[256]{0:T(256)S(1)} %add_rsqrt_fusion.1) | copy-start | bytes 3076
  88.1 60.5 %reduce-scatter.16.cloned.1.call-start = ((), (), s32[]{:S(2)}) async-start(), calls=%async_computation.12 | async-start | bytes 1966080 | tf_op jit(solution)/shard_map/reduce_scatter | solution.py:112
  107.9 3.3 copy-start.39
  111.1 5.4 copy-start.44
  120.4 29.8 %copy-start.4 = (bf16[1,256,768]{2,1,0:T(8,128)(2,1)S(1)}, bf16[1,256,768]{2,1,0:T(8,128)(2,1)}, u32[]{:S(2)}) copy-start(bf16[1,256,768]{2,1,0:T(8,128)(2,1)} %param.23) | copy-start | bytes 1179652
  120.4 29.8 %copy-start.30 = (f32[768]{0:T(1024)S(1)}, f32[768]{0:T(1024)}, u32[]{:S(2)}) copy-start(f32[768]{0:T(1024)} %param.21) | copy-start | bytes 9220
  120.4 51.6 %all-gather.9.cloned.1.call-start = ((), (), s32[]{:S(2)}) async-start(), calls=%async_computation.13 | async-start | bytes 1966080 | tf_op jit(solution)/shard_map/all_gather | solution.py:122
  152.2 68.6 %reduce-scatter.18.cloned.1.call-start = ((), (), s32[]{:S(2)}) async-start(), calls=%async_computation.14 | async-start | bytes 3932160 | tf_op jit(solution)/shard_map/reduce_scatter | solution.py:134
  172.0 5.5 copy-start.42
  177.5 2.2 copy-start.20
  182.8 38.1 %copy-start.38 = (f32[768]{0:T(1024)S(1)}, f32[768]{0:T(1024)}, u32[]{:S(2)}) copy-start(f32[768]{0:T(1024)} %param.22) | copy-start | bytes 9220
  182.8 41.2 %copy-start.27 = (f32[768]{0:T(1024)S(1)}, f32[768]{0:T(1024)}, u32[]{:S(2)}) copy-start(f32[768]{0:T(1024)} %param.19) | copy-start | bytes 9220
  182.8 62.8 %all-gather.11.cloned.1.call-start = ((), (), s32[]{:S(2)}) async-start(), calls=%async_computation.15 | async-start | bytes 1966080 | tf_op jit(solution)/shard_map/all_gather | solution.py:139
  224.0 21.6 %copy-start.25 = (bf16[192,768]{1,0:T(8,128)(2,1)S(1)}, bf16[192,768]{1,0:T(8,128)(2,1)}, u32[]{:S(2)}) copy-start(bf16[192,768]{1,0:T(8,128)(2,1)} %param.15) | copy-start | bytes 884740
  225.8 116.8 %reduce-scatter.30.cloned.1.call-start = ((), (), s32[]{:S(2)}) async-start(), calls=%async_computation.21 | async-start | bytes 884736
  247.7 6.3 slice-start
  247.7 7.3 %slice-start.1 = ((s8[12582912]{0:T(1024)(128)(4,1)}), s8[4194304]{0:T(1024)(128)(4,1)S(1)}, s32[]{:S(2)}) async-start(s8[12582912]{0:T(1024)(128)(4,1)} %bitcast.122), calls=%async_computation.23 | async-start | bytes 8388608
  247.7 8.5 %slice-start.2 = ((s8[12582912]{0:T(1024)(128)(4,1)}), s8[4194304]{0:T(1024)(128)(4,1)S(1)}, s32[]{:S(2)}) async-start(s8[12582912]{0:T(1024)(128)(4,1)} %bitcast.122), calls=%async_computation.24 | async-start | bytes 8388608
  256.2 5.3 copy-start.11
  256.2 5.3 copy-start.13
  261.4 5.0 copy-start.3
  261.4 5.0 copy-start.7
  261.5 5.0 copy-start.9
  269.6 93.1 %reduce-scatter.20.cloned.1.call-start = ((), (), s32[]{:S(2)}) async-start(), calls=%async_computation.16 | async-start | bytes 1966080 | tf_op jit(solution)/shard_map/reduce_scatter | solution.py:187
  270.0 6.7 %copy-start.43 = (bf16[768,3,192]{0,2,1:T(8,128)(2,1)S(1)}, bf16[768,3,192]{0,2,1:T(8,128)(2,1)}, u32[]{:S(2)}) copy-start(bf16[768,3,192]{0,2,1:T(8,128)(2,1)} %param.14) | copy-start | bytes 2654212
  279.3 154.0 %reduce-scatter.28.cloned.1.call-start = ((), (), s32[]{:S(2)}) async-start(), calls=%async_computation.20 | async-start | bytes 2211840
  283.1 3.3 copy-start.41
  286.1 219.9 %reduce-scatter.26.cloned.1.call-start = ((), (), s32[]{:S(2)}) async-start(), calls=%async_computation.19 | async-start | bytes 2654208 | tf_op jit(solution)/shard_map/reduce_scatter | solution.py:195
  290.7 288.0 %reduce-scatter.24.cloned.1.call-start = ((), (), s32[]{:S(2)}) async-start(), calls=%async_computation.18 | async-start | bytes 2654208 | tf_op jit(solution)/shard_map/reduce_scatter | solution.py:194
  296.4 355.1 %reduce-scatter.22.cloned.1.call-start = ((), (), s32[]{:S(2)}) async-start(), calls=%async_computation.17 | async-start | bytes 2654208 | tf_op jit(solution)/shard_map/reduce_scatter | solution.py:193
  302.1 349.4 %copy-start.1 = (bf16[768,768]{1,0:T(8,128)(2,1)S(1)}, bf16[768,768]{1,0:T(8,128)(2,1)}, u32[]{:S(2)}) copy-start(bf16[768,768]{1,0:T(8,128)(2,1)} %param.18) | copy-start | bytes 3538948
  (15 other events, 18.9 us)
Sparse Core Ops, SparseCore 0:
  9.6 22.3 all-gather.4
  47.6 37.8 reduce-scatter.13
  88.2 19.6 all-gather.6
  120.5 27.9 reduce-scatter.15
  152.3 19.6 all-gather.8
  182.9 37.8 reduce-scatter.17
  225.9 19.6 all-gather.10
  269.7 63.2 reduce-scatter.29
  335.5 27.1 reduce-scatter.19
  366.0 67.2 reduce-scatter.27
  437.4 68.5 reduce-scatter.25
  509.9 68.6 reduce-scatter.23
  582.7 68.7 reduce-scatter.21
where the time goes:
time: 659 us; the launch traced here: 658 us
  waiting for transfers between devices  489 us (74%)
  matrix products  72.9 us (11%)
  blocking collectives  39.8 us (6%)
  other arithmetic  21.7 us (3%)
  local copies, waits for them, and re-layouts  18.2 us (3%)
  between operations  15.1 us (2%)
    reduce_scatter x1, waiting for transfers between devices, body(): lax.psum_scatter(gate_grad, 'dp', scatter_dimension=0, tiled=True)  72.8 us
    reduce_scatter x1, waiting for transfers between devices, body(): lax.psum_scatter(up_grad, 'dp', scatter_dimension=0, tiled=True)  72.6 us
    reduce_scatter x1, waiting for transfers between devices, body(): lax.psum_scatter(down_grad, 'dp', scatter_dimension=1, tiled=True)  70.7 us
    unnamed x15, waiting for transfers between devices  69.5 us
    psum x1, blocking collectives, body(): lax.psum((gain_one_part, bias_one_part, gain_two_part, bias_two_part), ('...  39.8 us
    reduce_scatter x1, waiting for transfers between devices, body(): lax.psum_scatter(attn_partial, 'tp', scatter_dimension=1, tiled=True)  38 us
    reduce_scatter x1, waiting for transfers between devices, body(): lax.psum_scatter(grad_inner, 'tp', scatter_dimension=1, tiled=True)  38 us
    reduce_scatter x1, waiting for transfers between devices, body(): lax.psum_scatter(ffn_partial.astype(jnp.bfloat16), 'tp', scatter_dimensio...  27.9 us
  transfers between devices with their start and end apart: 13, of which 12 were waited for; matrix products, arithmetic and copies ran while one was open for 5% of the time, Pallas kernels for 0%

commit v1 on v0

--- a/solution.py
+++ b/solution.py
@@ -6,6 +6,19 @@
 HD = 64
 masked_score = -1e30
 epsilon = 1e-05
+
+
+def ring_gather(array, axis, dim):
+    ways = lax.axis_size(axis)
+    up = [(d, (d + 1) % ways) for d in range(ways)]
+    down = [(d, (d - 1) % ways) for d in range(ways)]
+    earlier, later = ([array], [array])
+    for _ in range(ways // 2):
+        earlier.append(lax.ppermute(earlier[-1], axis, up))
+    for _ in range((ways - 1) // 2):
+        later.append(lax.ppermute(later[-1], axis, down))
+    line = jnp.concatenate([*earlier[::-1], *later[1:]], axis=dim)
+    return jnp.roll(line, (lax.axis_index(axis) - ways // 2) * array.shape[dim], axis=dim)
 
 
 def angle_tables(positions_count, head_width):
@@ -71,7 +84,7 @@
     own_positions = offset + jnp.arange(piece_len, dtype=jnp.int32)
     row_valid = (own_positions[None, :] < lengths[:, None]).astype(jnp.float32)
     cosine, sine_table = angle_tables(seq_len, HD)
-    gathered = lax.all_gather(layer_input, "tp", axis=1, tiled=True)
+    gathered = ring_gather(layer_input, "tp", 1)
     projected = jnp.einsum("rsd,dce->rsce", gathered, w_qkv, preferred_element_type=jnp.float32)
     shaped = projected.reshape(row_count, seq_len, 3, heads_local, HD)
     queries = rotate(shaped[:, :, 0], cosine, sine_table, 1.0).astype(jnp.bfloat16)

time: 659 us -> 660 us (level)
    reduce_scatter x0 -> x1, waiting for transfers between devices: none -> 72.7 us  [body(): lax.psum_scatter(qkv_grad, 'dp', scatter_dimension=0, tiled=True)]
    unnamed x15 -> x13, waiting for transfers between devices: 69.5 us -> 0.2 us
    all_gather x1 -> x0, waiting for transfers between devices: 22.1 us -> none  [body(): gathered = lax.all_gather(layer_input, 'tp', axis=1, tiled=True)]
    ppermute x0 -> x3, waiting for transfers between devices: none -> 9.99 us  [the longest x2 9.99 us: ring_gather(): earlier.append(lax.ppermute(earlier[-1], axis, up))]
    unnamed x104 -> x120, local copies, waits for them, and re-layouts: 18.1 us -> 12.6 us
  transfers between devices with their start and end apart: 13 -> 15, of which waited for: 12 -> 13; matrix products, arithmetic and copies ran while one was open for 5% -> 5% of each run, Pallas kernels for 0% -> 0%
where the time goes in v1:
time: 660 us; the launch traced here: 659 us
  waiting for transfers between devices  490 us (74%)
  matrix products  73.3 us (11%)
  blocking collectives  39.8 us (6%)
  other arithmetic  21.7 us (3%)
  between operations  15.7 us (2%)
  local copies, waits for them, and re-layouts  12.8 us (2%)
    reduce_scatter x1, waiting for transfers between devices, body(): lax.psum_scatter(gate_grad, 'dp', scatter_dimension=0, tiled=True)  72.8 us
    reduce_scatter x1, waiting for transfers between devices, body(): lax.psum_scatter(qkv_grad, 'dp', scatter_dimension=0, tiled=True)  72.7 us
    reduce_scatter x1, waiting for transfers between devices, body(): lax.psum_scatter(up_grad, 'dp', scatter_dimension=0, tiled=True)  72.7 us
    reduce_scatter x1, waiting for transfers between devices, body(): lax.psum_scatter(down_grad, 'dp', scatter_dimension=1, tiled=True)  72 us
    reduce_scatter x1, waiting for transfers between devices, body(): lax.psum_scatter(attn_partial, 'tp', scatter_dimension=1, tiled=True)  41.8 us
    psum x1, blocking collectives, body(): lax.psum((gain_one_part, bias_one_part, gain_two_part, bias_two_part), ('...  39.8 us
    reduce_scatter x1, waiting for transfers between devices, body(): lax.psum_scatter(grad_inner, 'tp', scatter_dimension=1, tiled=True)  38 us
    reduce_scatter x1, waiting for transfers between devices, body(): lax.psum_scatter(ffn_partial.astype(jnp.bfloat16), 'tp', scatter_dimensio...  28.1 us
  transfers between devices with their start and end apart: 15, of which 13 were waited for; matrix products, arithmetic and copies ran while one was open for 5% of the time, Pallas kernels for 0%

profile of v1, /device:TPU:0, one launch (start us, length us, event | category | flops | bytes accessed | tf_op | source)
XLA Modules:
  0.0 659.0 jit_solution(965289056649639988)
XLA Ops:
  7.8 2.0 collective-permute-start.2
  9.8 7.2 %collective-permute-done = bf16[1,256,768]{2,1,0:T(8,128)(2,1)S(1)} collective-permute-done((bf16[1,256,768]{2,1,0:T(8,128)(2,1)}, bf16[1,256,768]{2,1,0:T(8,128)(2,1)S(1)}, u32[]{:S(2)}, u32[]{:S(2)}) %collective-permute-start) | collective-permute-done | bytes 393248 | tf_op jit(solution)/shard_map/ppermute | solution.py:17
  17.0 2.6 collective-permute-start.1
  20.2 1.2 broadcast_multiply_fusion
  21.5 2.8 collective-permute-done.1
  25.5 1.7 copy-done.36
  28.8 2.4 fusion.68
  31.2 1.7 fusion
  33.0 2.8 copy-done.2
  35.8 2.3 fusion.40
  38.9 2.3 convolution_bitcast_fusion
  41.2 41.8 %reduce-scatter.12.cloned.1.call-done = f32[1,256,768]{2,1,0:T(8,128)} async-done(((f32[1,1024,768]{2,1,0:T(8,128)}), f32[1,256,768]{2,1,0:T(8,128)}) %reduce-scatter.12.cloned.1.call-update) | async-done | bytes 786448 | tf_op jit(solution)/shard_map/reduce_scatter | solution.py:113
  83.0 1.3 fusion.67
  85.8 19.5 %all-gather.4.cloned.1.call-done = bf16[1,1024,768]{2,1,0:T(8,128)(2,1)} async-done(((bf16[1,256,768]{2,1,0:T(8,128)(2,1)}), bf16[1,1024,768]{2,1,0:T(8,128)(2,1)}) %all-gather.4.cloned.1.call-update) | async-done | bytes 1572880 | tf_op jit(solution)/shard_map/all_gather | solution.py:119
  105.4 3.3 fusion.23
  108.6 5.4 multiply_convert_fusion.3
  115.2 2.6 fusion.25
  117.9 28.1 %reduce-scatter.14.cloned.1.call-done = bf16[1,256,768]{2,1,0:T(8,128)(2,1)} async-done(((bf16[1,1024,768]{2,1,0:T(8,128)(2,1)}), bf16[1,256,768]{2,1,0:T(8,128)(2,1)}) %reduce-scatter.14.cloned.1.call-update) | async-done | bytes 393232 | tf_op jit(solution)/shard_map/reduce_scatter | solution.py:125
  146.0 1.3 fusion.66
  149.7 19.7 %all-gather.6.cloned.1.call-done = bf16[1,1024,768]{2,1,0:T(8,128)(2,1)} async-done(((bf16[1,256,768]{2,1,0:T(8,128)(2,1)}), bf16[1,1024,768]{2,1,0:T(8,128)(2,1)}) %all-gather.6.cloned.1.call-update) | async-done | bytes 1572880 | tf_op jit(solution)/shard_map/all_gather | solution.py:135
  169.4 5.4 multiply_convert_fusion.1
  174.9 1.4 fusion.69
  177.0 3.1 add_bitcast_fusion
  180.3 38.0 %reduce-scatter.16.cloned.1.call-done = f32[1,256,768]{2,1,0:T(8,128)} async-done(((f32[1,1024,768]{2,1,0:T(8,128)}), f32[1,256,768]{2,1,0:T(8,128)}) %reduce-scatter.16.cloned.1.call-update) | async-done | bytes 786448 | tf_op jit(solution)/shard_map/reduce_scatter | solution.py:147
  218.2 3.2 multiply_reduce_fusion.2
  221.4 1.7 fusion.64
  223.5 19.5 %all-gather.8.cloned.1.call-done = bf16[1,1024,768]{2,1,0:T(8,128)(2,1)} async-done(((bf16[1,256,768]{2,1,0:T(8,128)(2,1)}), bf16[1,1024,768]{2,1,0:T(8,128)(2,1)}) %all-gather.8.cloned.1.call-update) | async-done | bytes 1572880 | tf_op jit(solution)/shard_map/all_gather | solution.py:152
  242.9 2.1 fusion.34
  245.0 6.3 multiply_reduce_fusion
  252.3 1.2 slice-done.2
  253.5 5.3 multiply_convert_fusion
  258.8 5.0 fusion.29
  263.8 1.2 fusion.30
  265.3 1.6 fusion.31
  267.3 6.9 %fusion.37 = bf16[3,64,1024]{2,1,0:T(8,128)(2,1)S(1)} fusion(bf16[1024,3,64]{0,2,1:T(8,128)(2,1)S(1)} %bitcast.121, f32[3,1024,1024]{1,2,0:T(8,128)} %copy-done.2, f32[3,1024]{1,0:T(4,128)S(1)} %log_add_fusion), kind=kOutput, calls=%fused_computation.49 | convolution fusion | flops 409141248 | bytes 13381632 | tf_op jit(solution)/shard_map/while/body/eval_jaxpr/hst,she->the/dot_general | solution.py:178
  274.2 2.6 fusion.26
  276.9 4.9 fusion.13
  282.1 4.3 fusion.17
  286.6 4.9 fusion.19
  291.6 4.4 fusion.6
  296.1 39.8 %all-reduce = (f32[768]{0:T(1024)}, f32[768]{0:T(1024)}, f32[768]{0:T(1024)}, f32[768]{0:T(1024)}) all-reduce(f32[768]{0:T(1024)S(1)} %copy-done.43, f32[768]{0:T(1024)S(1)} %copy-done.44, f32[768]{0:T(1024)S(1)} %copy-done.41, f32[768]{0:T(1024)S(1)} %copy-done.42), channel_id=1, replica_groups=mesh['dp'=8,'tp'=4] {'dp','tp'}, use_global_device_ids=true, to_apply=%region_21.22 | all-reduce | flops 3072 | bytes 24576 | tf_op jit(solution)/shard_map/psum | solution.py:210
  335.9 1.6 copy.41
  337.5 22.5 %reduce-scatter.18.cloned.1.call-done = bf16[1,256,768]{2,1,0:T(8,128)(2,1)} async-done(((bf16[1,1024,768]{2,1,0:T(8,128)(2,1)}), bf16[1,256,768]{2,1,0:T(8,128)(2,1)}) %reduce-scatter.18.cloned.1.call-update) | async-done | bytes 393232 | tf_op jit(solution)/shard_map/reduce_scatter | solution.py:200
  360.0 1.9 convert_add_fusion
  361.9 72.0 %reduce-scatter.26.cloned.1.call-done = f32[768,96]{0,1:T(8,128)} async-done(((f32[768,768]{0,1:T(8,128)}), f32[768,96]{0,1:T(8,128)}) %reduce-scatter.26.cloned.1.call-update) | async-done | bytes 294928 | tf_op jit(solution)/shard_map/reduce_scatter | solution.py:208
  433.9 72.7 %reduce-scatter.24.cloned.1.call-done = f32[96,768]{1,0:T(8,128)} async-done(((f32[768,768]{1,0:T(8,128)}), f32[96,768]{1,0:T(8,128)}) %reduce-scatter.24.cloned.1.call-update) | async-done | bytes 294928 | tf_op jit(solution)/shard_map/reduce_scatter | solution.py:207
  506.6 72.8 %reduce-scatter.22.cloned.1.call-done = f32[96,768]{1,0:T(8,128)} async-done(((f32[768,768]{1,0:T(8,128)}), f32[96,768]{1,0:T(8,128)}) %reduce-scatter.22.cloned.1.call-update) | async-done | bytes 294928 | tf_op jit(solution)/shard_map/reduce_scatter | solution.py:206
  579.4 72.7 %reduce-scatter.20.cloned.1.call-done = f32[96,3,192]{2,0,1:T(8,128)} async-done(((f32[768,3,192]{2,0,1:T(8,128)}), f32[96,3,192]{2,0,1:T(8,128)}) %reduce-scatter.20.cloned.1.call-update) | async-done | bytes 221200 | tf_op jit(solution)/shard_map/reduce_scatter | solution.py:204
  (167 shorter events, 12.5 us)
Async XLA Ops:
  7.2 108.0 %copy-start = (bf16[768,768]{1,0:T(8,128)(2,1)S(1)}, bf16[768,768]{1,0:T(8,128)(2,1)}, u32[]{:S(2)}) copy-start(bf16[768,768]{1,0:T(8,128)(2,1)} %param.18) | copy-start | bytes 3538948
  7.2 18.3 %copy-start.4 = (bf16[1,256,768]{2,1,0:T(8,128)(2,1)S(1)}, bf16[1,256,768]{2,1,0:T(8,128)(2,1)}, u32[]{:S(2)}) copy-start(bf16[1,256,768]{2,1,0:T(8,128)(2,1)} %param.12) | copy-start | bytes 1179652
  7.2 75.8 %reduce-scatter.12.cloned.1.call-start = ((), (), s32[]{:S(2)}) async-start(), calls=%async_computation.9 | async-start | bytes 3932160 | tf_op jit(solution)/shard_map/reduce_scatter | solution.py:113
  7.3 9.8 %collective-permute-start = (bf16[1,256,768]{2,1,0:T(8,128)(2,1)}, bf16[1,256,768]{2,1,0:T(8,128)(2,1)S(1)}, u32[]{:S(2)}, u32[]{:S(2)}) collective-permute-start(bf16[1,256,768]{2,1,0:T(8,128)(2,1)} %param.12), channel_id=1, source_target_pairs={{0,1},{1,2},{2,3},{3,0},{4,5},{5,6},{6,7},{7,4},{8,9},{9,10},{10,1... | collective-permute-start | bytes 1179656 | tf_op jit(solution)/shard_map/ppermute | solution.py:17
  7.8 17.5 %collective-permute-start.2 = (bf16[1,256,768]{2,1,0:T(8,128)(2,1)}, bf16[1,256,768]{2,1,0:T(8,128)(2,1)S(1)}, u32[]{:S(2)}, u32[]{:S(2)}) collective-permute-start(bf16[1,256,768]{2,1,0:T(8,128)(2,1)} %param.12), channel_id=1, source_target_pairs={{0,3},{1,0},{2,1},{3,2},{4,7},{5,4},{6,5},{7,6},{8,11},{9,8},{10,9... | collective-permute-start | bytes 1179656 | tf_op jit(solution)/shard_map/ppermute | solution.py:19
  17.0 7.2 %collective-permute-start.1 = (bf16[1,256,768]{2,1,0:T(8,128)(2,1)S(1)}, bf16[1,256,768]{2,1,0:T(8,128)(2,1)S(1)}, u32[]{:S(2)}, u32[]{:S(2)}) collective-permute-start(bf16[1,256,768]{2,1,0:T(8,128)(2,1)S(1)} %collective-permute-done), channel_id=1, source_target_pairs={{0,1},{1,2},{2,3},{3,0},{4,5},{5,6},{6,7},{7,4},{8,9},{9,10},{10,1... | collective-permute-start | bytes 1179656 | tf_op jit(solution)/shard_map/ppermute | solution.py:17
  21.5 7.1 %copy-start.21 = (f32[1024,32]{0,1:T(8,128)}, f32[1024,32]{0,1:T(8,128)S(1)}, u32[]{:S(2)}) copy-start(f32[1024,32]{0,1:T(8,128)S(1)} %get-tuple-element.100) | copy-start | bytes 393220
  21.5 5.8 copy-start.48
  28.3 4.7 copy-start.6
  41.1 43.4 %copy-start.32 = (f32[768]{0:T(1024)S(1)}, f32[768]{0:T(1024)}, u32[]{:S(2)}) copy-start(f32[768]{0:T(1024)} %param.19) | copy-start | bytes 9220
  41.1 43.5 %copy-start.40 = (f32[768]{0:T(1024)S(1)}, f32[768]{0:T(1024)}, u32[]{:S(2)}) copy-start(f32[768]{0:T(1024)} %param.20) | copy-start | bytes 9220
  41.2 64.2 %all-gather.4.cloned.1.call-start = ((), (), s32[]{:S(2)}) async-start(), calls=%async_computation.10 | async-start | bytes 1966080 | tf_op jit(solution)/shard_map/all_gather | solution.py:119
  84.3 133.9 %copy-start.38 = (f32[256]{0:T(256)}, f32[256]{0:T(256)S(1)}, u32[]{:S(2)}) copy-start(f32[256]{0:T(256)S(1)} %broadcast_multiply_fusion.6) | copy-start | bytes 3076
  84.6 133.6 %copy-start.39 = (f32[256]{0:T(256)}, f32[256]{0:T(256)S(1)}, u32[]{:S(2)}) copy-start(f32[256]{0:T(256)S(1)} %add_rsqrt_fusion.1) | copy-start | bytes 3076
  85.6 60.4 %reduce-scatter.14.cloned.1.call-start = ((), (), s32[]{:S(2)}) async-start(), calls=%async_computation.11 | async-start | bytes 1966080 | tf_op jit(solution)/shard_map/reduce_scatter | solution.py:125
  108.6 5.4 copy-start.50
  117.8 29.8 %copy-start.5 = (bf16[1,256,768]{2,1,0:T(8,128)(2,1)S(1)}, bf16[1,256,768]{2,1,0:T(8,128)(2,1)}, u32[]{:S(2)}) copy-start(bf16[1,256,768]{2,1,0:T(8,128)(2,1)} %param.23) | copy-start | bytes 1179652
  117.8 29.8 %copy-start.37 = (f32[768]{0:T(1024)S(1)}, f32[768]{0:T(1024)}, u32[]{:S(2)}) copy-start(f32[768]{0:T(1024)} %param.21) | copy-start | bytes 9220
  117.8 51.6 %all-gather.6.cloned.1.call-start = ((), (), s32[]{:S(2)}) async-start(), calls=%async_computation.12 | async-start | bytes 1966080 | tf_op jit(solution)/shard_map/all_gather | solution.py:135
  149.6 68.6 %reduce-scatter.16.cloned.1.call-start = ((), (), s32[]{:S(2)}) async-start(), calls=%async_computation.13 | async-start | bytes 3932160 | tf_op jit(solution)/shard_map/reduce_scatter | solution.py:147
  169.4 5.5 copy-start.47
  180.2 38.1 %copy-start.45 = (f32[768]{0:T(1024)S(1)}, f32[768]{0:T(1024)}, u32[]{:S(2)}) copy-start(f32[768]{0:T(1024)} %param.22) | copy-start | bytes 9220
  180.2 41.3 %copy-start.33 = (f32[768]{0:T(1024)S(1)}, f32[768]{0:T(1024)}, u32[]{:S(2)}) copy-start(f32[768]{0:T(1024)} %param.19) | copy-start | bytes 9220
  180.2 43.2 %copy-start.35 = (f32[3,1024]{1,0:T(4,128)S(1)}, f32[3,1024]{1,0:T(4,128)}, u32[]{:S(2)}) copy-start(f32[3,1024]{1,0:T(4,128)} %copy-done.34) | copy-start | bytes 36868
  180.2 62.7 %copy-start.31 = (bf16[192,768]{1,0:T(8,128)(2,1)S(1)}, bf16[192,768]{1,0:T(8,128)(2,1)}, u32[]{:S(2)}) copy-start(bf16[192,768]{1,0:T(8,128)(2,1)} %param.15) | copy-start | bytes 884740
  180.2 62.7 %all-gather.8.cloned.1.call-start = ((), (), s32[]{:S(2)}) async-start(), calls=%async_computation.14 | async-start | bytes 1966080 | tf_op jit(solution)/shard_map/all_gather | solution.py:152
  223.2 112.7 %reduce-scatter.28.cloned.1.call-start = ((), (), s32[]{:S(2)}) async-start(), calls=%async_computation.20 | async-start | bytes 884736
  245.0 6.3 slice-start
  245.0 7.3 %slice-start.1 = ((s8[12582912]{0:T(1024)(128)(4,1)}), s8[4194304]{0:T(1024)(128)(4,1)S(1)}, s32[]{:S(2)}) async-start(s8[12582912]{0:T(1024)(128)(4,1)} %bitcast.118), calls=%async_computation.22 | async-start | bytes 8388608
  245.0 8.5 %slice-start.2 = ((s8[12582912]{0:T(1024)(128)(4,1)}), s8[4194304]{0:T(1024)(128)(4,1)S(1)}, s32[]{:S(2)}) async-start(s8[12582912]{0:T(1024)(128)(4,1)} %bitcast.118), calls=%async_computation.23 | async-start | bytes 8388608
  253.5 5.3 copy-start.12
  253.5 5.3 copy-start.14
  258.8 5.0 copy-start.3
  258.8 5.0 copy-start.8
  258.8 5.0 copy-start.10
  266.9 93.1 %reduce-scatter.18.cloned.1.call-start = ((), (), s32[]{:S(2)}) async-start(), calls=%async_computation.15 | async-start | bytes 1966080 | tf_op jit(solution)/shard_map/reduce_scatter | solution.py:200
  267.3 6.9 %copy-start.26 = (bf16[1,1024,3,64]{1,3,2,0:T(8,128)(2,1)}, bf16[1,1024,3,64]{1,3,2,0:T(8,128)(2,1)S(1)}, u32[]{:S(2)}) copy-start(bf16[1,1024,3,64]{1,3,2,0:T(8,128)(2,1)S(1)} %pad_maximum_fusion.5) | copy-start | bytes 1179652
  267.3 6.9 %copy-start.28 = (bf16[1,1024,3,64]{1,3,2,0:T(8,128)(2,1)}, bf16[1,1024,3,64]{1,3,2,0:T(8,128)(2,1)S(1)}, u32[]{:S(2)}) copy-start(bf16[1,1024,3,64]{1,3,2,0:T(8,128)(2,1)S(1)} %pad_maximum_fusion.6) | copy-start | bytes 1179652
  267.3 6.9 %copy-start.49 = (bf16[768,3,192]{0,2,1:T(8,128)(2,1)S(1)}, bf16[768,3,192]{0,2,1:T(8,128)(2,1)}, u32[]{:S(2)}) copy-start(bf16[768,3,192]{0,2,1:T(8,128)(2,1)} %param.14) | copy-start | bytes 2654212
  276.9 5.2 copy-start.19
  276.9 157.0 %reduce-scatter.26.cloned.1.call-start = ((), (), s32[]{:S(2)}) async-start(), calls=%async_computation.19 | async-start | bytes 2654208 | tf_op jit(solution)/shard_map/reduce_scatter | solution.py:208
  281.8 224.8 %reduce-scatter.24.cloned.1.call-start = ((), (), s32[]{:S(2)}) async-start(), calls=%async_computation.18 | async-start | bytes 2654208 | tf_op jit(solution)/shard_map/reduce_scatter | solution.py:207
  286.5 5.1 copy-start.25
  286.5 5.1 copy-start.27
  286.5 5.1 copy-start.29
  286.5 292.9 %reduce-scatter.22.cloned.1.call-start = ((), (), s32[]{:S(2)}) async-start(), calls=%async_computation.17 | async-start | bytes 2654208 | tf_op jit(solution)/shard_map/reduce_scatter | solution.py:206
  291.5 360.6 %reduce-scatter.20.cloned.1.call-start = ((), (), s32[]{:S(2)}) async-start(), calls=%async_computation.16 | async-start | bytes 2654208 | tf_op jit(solution)/shard_map/reduce_scatter | solution.py:204
  291.6 360.5 %copy-start.1 = (bf16[768,768]{1,0:T(8,128)(2,1)S(1)}, bf16[768,768]{1,0:T(8,128)(2,1)}, u32[]{:S(2)}) copy-start(bf16[768,768]{1,0:T(8,128)(2,1)} %param.18) | copy-start | bytes 3538948
  (23 other events, 59.0 us)
Sparse Core Ops, SparseCore 0:
  41.3 41.7 reduce-scatter.11
  85.7 19.6 all-gather.3
  117.9 27.9 reduce-scatter.13
  149.8 19.6 all-gather.5
  180.3 37.8 reduce-scatter.15
  223.3 19.6 all-gather.7
  267.1 63.2 reduce-scatter.27
  332.9 27.0 reduce-scatter.17
  364.1 69.7 reduce-scatter.25
  437.8 68.7 reduce-scatter.23
  510.7 68.7 reduce-scatter.21
  583.3 68.7 reduce-scatter.19
